TPU v7x, 32 devices: a whole 2x2x4 slice. The times are simulated.
32 devices in a mesh: parts: 2 (over y), wide: 4 (over z), narrow: 4 (over x, core).
Axes of the slice: x: 2, y: 2, z: 4, core: 2. Of those that a mesh axis runs over, the one named last changes fastest.
Arguments:
- embeddings: bfloat16 [8192, 1024], P(('parts', 'wide', 'narrow')), parts along dimension 0, may hold values from -6 to 6
- cluster_id: int32 [8192], P(('parts', 'wide', 'narrow')), parts along dimension 0, may hold values from 0 to 63, as said below
- order_index: int32 [8192], P(('parts', 'wide', 'narrow')), parts along dimension 0, may hold values from 0 to 2047, as said below
Outputs:
- nearest: float32 [8192], P(('parts', 'wide', 'narrow')), parts along dimension 0
There are 2 independent parts, one for each index of `parts`. A program takes and returns all parts, laid end to end along the dimension named above; each array names one. Nothing has to cross between parts.
Inputs may be any that keep to these rules, and one draw needn't show every extreme that they name: `cluster_id`: cluster c belongs to owner c // 16 of wide; among the members held by one device at most 128 belong to clusters of one owner, and in every draw one owner gets exactly 128 from every device. `order_index`: the members of each cluster carry the distinct numbers 0, 1, 2, ... up to its size less one; in every draw some cluster holds 4 * 4 * 128 members.
All inputs are finite; a program needn't handle non-finite values.
Results may differ from a plain program's by a relative error of at most 0.00099.
Values may be sent and summed in bfloat16 or wider, within the bound.
A program may use at most 64 MiB of HBM per device.

v0:
```python
import jax
import jax.numpy as jnp
from jax import lax
from jax.sharding import PartitionSpec as P

CPO = 16


def shifted(shard, axis, by):
    count = lax.axis_size(axis)
    return lax.ppermute(shard, axis, [(i, (i + by) % count) for i in range(count)])


def pair_inner(left, right):
    return lax.dot_general(
        left, right, (((1,), (1,)), ((), ())), preferred_element_type=jnp.float32
    )


def per_device(embeddings, cluster_id, order_index):
    wide_size = lax.axis_size("wide")
    rows = embeddings.shape[0]
    width = embeddings.shape[1]
    bucket = 2 * rows // wide_size
    values = embeddings.astype(jnp.float32)
    unit = (values * lax.rsqrt(jnp.sum(values * values, axis=1, keepdims=True) + 1e-06)).astype(
        jnp.bfloat16
    )
    owner = cluster_id // CPO
    owner_hot = (owner[:, None] == jnp.arange(wide_size, dtype=jnp.int32)[None, :]).astype(
        jnp.int32
    )
    earlier = jnp.cumsum(owner_hot, axis=0) - owner_hot
    slot = jnp.sum(earlier * owner_hot, axis=1)
    target = owner * bucket + slot
    send_rows = jnp.zeros((wide_size * bucket, width), jnp.bfloat16).at[target].set(unit)
    meta_rows = jnp.stack([cluster_id, order_index], axis=1)
    send_meta = jnp.full((wide_size * bucket, 2), -1, jnp.int32).at[target].set(meta_rows)
    held, held_meta = (
        lax.all_to_all(send_rows, "wide", split_axis=0, concat_axis=0, tiled=True),
        lax.all_to_all(send_meta, "wide", split_axis=0, concat_axis=0, tiled=True),
    )
    held_cl = held_meta[:, 0]
    held_or = held_meta[:, 1]
    live = held_cl >= 0
    start_best = jnp.full((held.shape[0],), -1.0, jnp.float32)

    def row_best(inner, other_cl, other_or):
        allowed = (
            (other_cl[None, :] == held_cl[:, None])
            & (other_or[None, :] < held_or[:, None])
            & live[:, None]
        )
        return jnp.max(jnp.where(allowed, inner, -1.0), axis=1)

    narrow_size = lax.axis_size("narrow")
    best = jnp.maximum(start_best, row_best(pair_inner(held, held), held_cl, held_or))
    for distance in range(1, narrow_size // 2 + 1):
        other_rows, other_meta = shifted((held, held_meta), "narrow", distance)
        other_cl = other_meta[:, 0]
        other_or = other_meta[:, 1]
        inner = pair_inner(held, other_rows)
        best = jnp.maximum(best, row_best(inner, other_cl, other_or))
        column_ok = (
            (held_cl[:, None] == other_cl[None, :])
            & (held_or[:, None] < other_or[None, :])
            & (other_cl[None, :] >= 0)
        )
        column_best = jnp.max(jnp.where(column_ok, inner, -1.0), axis=0)
        returned = shifted(column_best, "narrow", -distance)
        best = jnp.maximum(best, returned)
    answers = lax.all_to_all(best, "wide", split_axis=0, concat_axis=0, tiled=True)
    return answers[target]


def solution(mesh):
    return jax.shard_map(
        per_device,
        mesh=mesh,
        in_specs=(
            P(("parts", "wide", "narrow"), None),
            P(("parts", "wide", "narrow")),
            P(("parts", "wide", "narrow")),
        ),
        out_specs=P(("parts", "wide", "narrow")),
        check_vma=False,
    )
```

profile of v0, /device:TPU:0, one launch (start us, length us, event | category | flops | bytes accessed | tf_op | source)
XLA Modules:
  0.0 90.3 jit_solution(16906391178311085713)
XLA Ops:
  0.0 0.0 copy-start.1
  0.0 0.0 copy-start
  0.0 0.8 fusion.22
  0.8 0.0 copy-done.1
  0.8 1.2 %reduce-window.6 = s32[4,2,128]{2,1,0:T(2,128)S(1)} reduce-window(s32[4,2,128]{2,1,0:T(2,128)S(1)} %compare_convert_fusion, s32[]{:T(128)} %constant.14.clone.1), window={size=1x1x128 pad=0_0x0_0x127_0}, to_apply=%region_0.0 | reduce-window | flops 130048 | bytes 8196 | tf_op jit(solution)/shard_map/reduce-window
  2.0 0.1 slice.34
  2.1 0.1 copy.24
  2.2 0.1 copy.25
  2.3 0.1 add_bitcast_fusion
  2.5 1.2 %fusion.1 = f32[256]{0:T(256)S(1)} fusion(bf16[256,1024]{1,0:T(8,128)(2,1)} %param.3), kind=kLoop, calls=%fused_computation.7 | loop fusion | flops 786176 | bytes 525312 | tf_op jit(solution)/shard_map/reduce_sum | solution.py:26
  3.7 0.0 copy-done
  3.7 2.0 %scatter_custom_fusion.1 = bf16[512,1024]{1,0:T(8,128)(2,1)S(1)} fusion(s32[256]{0:T(256)S(1)} %compare_select_fusion, bf16[256,1024]{1,0:T(8,128)(2,1)S(1)} %copy-done, f32[256]{0:T(256)S(1)} %add_rsqrt_fusion, bf16[]{:T(256)} %constant.35.clone.1), kind=kCustom, calls=%fused_computation.13 | custom fusion | flops 786432 | bytes 1573890 | tf_op jit(solution)/shard_map/scatter | solution.py:36
  5.7 31.9 %all_to_all.36 = bf16[4,128,1024]{2,1,0:T(8,128)(2,1)S(1)} all-to-all(bf16[4,128,1024]{2,1,0:T(8,128)(2,1)S(1)} %bitcast.44), channel_id=1, replica_groups=mesh['parts'=2,'wide'=4,'narrow'=4] {'wide'}, dimensions={0} | all-to-all | bytes 2097152 | tf_op jit(solution)/shard_map/all_to_all | solution.py:40
  37.6 1.5 %collective-permute-start.4 = (bf16[512,1024]{1,0:T(8,128)(2,1)S(1)}, bf16[512,1024]{1,0:T(8,128)(2,1)S(1)}, u32[]{:S(2)}, u32[]{:S(2)}) collective-permute-start(bf16[512,1024]{1,0:T(8,128)(2,1)S(1)} %bitcast.45), channel_id=1, source_target_pairs={{0,2},{1,3},{2,0},{3,1},{4,6},{5,7},{6,4},{7,5},{8,10},{9,11},{10,... | collective-permute-start | bytes 3145736 | tf_op jit(solution)/shard_map/ppermute | solution.py:11
  39.0 0.0 copy-start.2
  39.0 0.7 copy-done.2
  39.7 0.1 copy.26
  39.9 1.2 %scatter_custom_fusion = s32[512,2]{1,0:T(8,128)S(1)} fusion(s32[256]{0:T(256)S(1)} %compare_select_fusion, s32[256,2]{1,0:T(8,128)S(1)} %copy.26, s32[]{:T(128)} %constant.12.clone.1), kind=kCustom, calls=%fused_computation.16 | custom fusion | bytes 4100 | tf_op jit(solution)/shard_map/scatter | solution.py:38
  41.1 0.1 copy.27
  41.2 8.1 %all_to_all.37 = s32[4,128,2]{1,2,0:T(2,128)S(1)} all-to-all(s32[4,128,2]{1,2,0:T(2,128)S(1)} %copy.27), channel_id=1, replica_groups=mesh['parts'=2,'wide'=4,'narrow'=4] {'wide'}, dimensions={0} | all-to-all | bytes 8192 | tf_op jit(solution)/shard_map/all_to_all | solution.py:41
  49.3 0.0 collective-permute-start
  49.3 0.6 collective-permute-start.1
  50.0 1.6 %collective-permute-start.3 = (s32[512,2]{0,1:T(2,128)S(1)}, s32[512,2]{0,1:T(2,128)S(1)}, u32[]{:S(2)}, u32[]{:S(2)}) collective-permute-start(s32[512,2]{0,1:T(2,128)S(1)} %bitcast.54), channel_id=1, source_target_pairs={{0,2},{1,3},{2,0},{3,1},{4,6},{5,7},{6,4},{7,5},{8,10},{9,11},{10,... | collective-permute-start | bytes 12296 | tf_op jit(solution)/shard_map/ppermute | solution.py:11
  51.6 7.7 %collective-permute-done = s32[512,2]{0,1:T(2,128)S(1)} collective-permute-done((s32[512,2]{0,1:T(2,128)S(1)}, s32[512,2]{0,1:T(2,128)S(1)}, u32[]{:S(2)}, u32[]{:S(2)}) %collective-permute-start) | collective-permute-done | bytes 4128 | tf_op jit(solution)/shard_map/ppermute | solution.py:11
  59.3 4.4 %collective-permute-done.3 = s32[512,2]{0,1:T(2,128)S(1)} collective-permute-done((s32[512,2]{0,1:T(2,128)S(1)}, s32[512,2]{0,1:T(2,128)S(1)}, u32[]{:S(2)}, u32[]{:S(2)}) %collective-permute-start.3) | collective-permute-done | bytes 4128 | tf_op jit(solution)/shard_map/ppermute | solution.py:11
  63.7 0.0 collective-permute-done.4
  63.7 0.7 fusion.15
  64.5 8.2 %collective-permute-done.1 = bf16[512,1024]{1,0:T(8,128)(2,1)S(1)} collective-permute-done((bf16[512,1024]{1,0:T(8,128)(2,1)S(1)}, bf16[512,1024]{1,0:T(8,128)(2,1)S(1)}, u32[]{:S(2)}, u32[]{:S(2)}) %collective-permute-start.1) | collective-permute-done | bytes 1048608 | tf_op jit(solution)/shard_map/ppermute | solution.py:11
  72.7 2.0 %select_reduce_fusion.3 = (f32[512]{0:T(512)S(1)}, f32[512]{0:T(512)S(1)}, f32[512]{0:T(512)S(1)}, f32[512]{0:T(512)S(1)}) fusion(s32[512]{0:T(512)S(1)} %bitcast.63, s32[512]{0:T(512)S(1)} %bitcast.61, s32[512]{0:T(512)S(1)} %bitcast.65, s32[512]{0:T(512)S(1)} %bitcast.57, pred[512]{0:T(512)(128)(4,1)S(1)} %compare_reduce_fusion, ...), kind=kOutput, calls=%fused_computation.12 | convolution fusion | flops 543160320 | bytes 3167744 | tf_op jit(solution)/shard_map/dot_general | solution.py:15
  74.7 1.6 %collective-permute-start.5 = (f32[512]{0:T(512)S(1)}, f32[512]{0:T(512)S(1)}, u32[]{:S(2)}, u32[]{:S(2)}) collective-permute-start(f32[512]{0:T(512)S(1)} %get-tuple-element.9), channel_id=1, source_target_pairs={{0,2},{1,3},{2,0},{3,1},{4,6},{5,7},{6,4},{7,5},{8,10},{9,11},{10,... | collective-permute-start | bytes 6152 | tf_op jit(solution)/shard_map/ppermute | solution.py:11
  76.3 0.8 collective-permute-start.2
  77.1 0.8 fusion
  77.9 0.4 collective-permute-done.5
  78.4 0.0 collective-permute-done.2
  78.4 0.6 maximum_maximum_fusion
  79.0 3.4 %all-to-all-start.2 = ((f32[4,128,1]{1,2,0:T(1,128)}), f32[4,128,1]{1,2,0:T(1,128)S(1)}, u32[]{:S(2)}, u32[]{:S(2)}) async-start(f32[4,128,1]{1,2,0:T(1,128)} %bitcast.16), calls=%async_computation.2 | async-start | bytes 4096 | tf_op jit(solution)/shard_map/all_to_all | solution.py:72
  82.4 5.4 %all-to-all-done.2 = f32[4,128,1]{1,2,0:T(1,128)S(1)} async-done(((f32[4,128,1]{1,2,0:T(1,128)}), f32[4,128,1]{1,2,0:T(1,128)S(1)}, u32[]{:S(2)}, u32[]{:S(2)}) %all-to-all-start.2) | async-done | bytes 2080 | tf_op jit(solution)/shard_map/all_to_all | solution.py:72
  87.8 2.5 %gather_fusion = f32[256]{0:T(256)} fusion(f32[512]{0:T(512)S(1)} %bitcast.43, s32[1024]{0:T(1024)S(1)} %pad_clamp_fusion), kind=kCustom, calls=%fused_computation | custom fusion | bytes 3072 | tf_op jit(solution)/shard_map/gather | solution.py:73
  (14 shorter events, 0.2 us)
Async XLA Ops:
  0.0 0.8 copy-start.1
  0.0 3.7 %copy-start = (bf16[256,1024]{1,0:T(8,128)(2,1)S(1)}, bf16[256,1024]{1,0:T(8,128)(2,1)}, u32[]{:S(2)}) copy-start(bf16[256,1024]{1,0:T(8,128)(2,1)} %param.3) | copy-start | bytes 1572868
  37.6 26.1 %collective-permute-start.4 = (bf16[512,1024]{1,0:T(8,128)(2,1)S(1)}, bf16[512,1024]{1,0:T(8,128)(2,1)S(1)}, u32[]{:S(2)}, u32[]{:S(2)}) collective-permute-start(bf16[512,1024]{1,0:T(8,128)(2,1)S(1)} %bitcast.45), channel_id=1, source_target_pairs={{0,2},{1,3},{2,0},{3,1},{4,6},{5,7},{6,4},{7,5},{8,10},{9,11},{10,... | collective-permute-start | bytes 3145736 | tf_op jit(solution)/shard_map/ppermute | solution.py:11
  39.0 0.7 copy-start.2
  49.3 9.9 %collective-permute-start = (s32[512,2]{0,1:T(2,128)S(1)}, s32[512,2]{0,1:T(2,128)S(1)}, u32[]{:S(2)}, u32[]{:S(2)}) collective-permute-start(s32[512,2]{0,1:T(2,128)S(1)} %bitcast.51), channel_id=1, source_target_pairs={{0,1},{1,2},{2,3},{3,0},{4,5},{5,6},{6,7},{7,4},{8,9},{9,10},{10,1... | collective-permute-start | bytes 12296 | tf_op jit(solution)/shard_map/ppermute | solution.py:11
  49.3 23.4 %collective-permute-start.1 = (bf16[512,1024]{1,0:T(8,128)(2,1)S(1)}, bf16[512,1024]{1,0:T(8,128)(2,1)S(1)}, u32[]{:S(2)}, u32[]{:S(2)}) collective-permute-start(bf16[512,1024]{1,0:T(8,128)(2,1)S(1)} %bitcast.46), channel_id=1, source_target_pairs={{0,1},{1,2},{2,3},{3,0},{4,5},{5,6},{6,7},{7,4},{8,9},{9,10},{10,1... | collective-permute-start | bytes 3145736 | tf_op jit(solution)/shard_map/ppermute | solution.py:11
  50.0 13.7 %collective-permute-start.3 = (s32[512,2]{0,1:T(2,128)S(1)}, s32[512,2]{0,1:T(2,128)S(1)}, u32[]{:S(2)}, u32[]{:S(2)}) collective-permute-start(s32[512,2]{0,1:T(2,128)S(1)} %bitcast.54), channel_id=1, source_target_pairs={{0,2},{1,3},{2,0},{3,1},{4,6},{5,7},{6,4},{7,5},{8,10},{9,11},{10,... | collective-permute-start | bytes 12296 | tf_op jit(solution)/shard_map/ppermute | solution.py:11
  74.7 3.7 %collective-permute-start.5 = (f32[512]{0:T(512)S(1)}, f32[512]{0:T(512)S(1)}, u32[]{:S(2)}, u32[]{:S(2)}) collective-permute-start(f32[512]{0:T(512)S(1)} %get-tuple-element.9), channel_id=1, source_target_pairs={{0,2},{1,3},{2,0},{3,1},{4,6},{5,7},{6,4},{7,5},{8,10},{9,11},{10,... | collective-permute-start | bytes 6152 | tf_op jit(solution)/shard_map/ppermute | solution.py:11
  76.3 2.1 %collective-permute-start.2 = (f32[512]{0:T(512)S(1)}, f32[512]{0:T(512)S(1)}, u32[]{:S(2)}, u32[]{:S(2)}) collective-permute-start(f32[512]{0:T(512)S(1)} %get-tuple-element.6), channel_id=1, source_target_pairs={{0,3},{1,0},{2,1},{3,2},{4,7},{5,4},{6,5},{7,6},{8,11},{9,8},{10,9... | collective-permute-start | bytes 6152 | tf_op jit(solution)/shard_map/ppermute | solution.py:11
  79.0 8.8 %all-to-all-start.2 = ((f32[4,128,1]{1,2,0:T(1,128)}), f32[4,128,1]{1,2,0:T(1,128)S(1)}, u32[]{:S(2)}, u32[]{:S(2)}) async-start(f32[4,128,1]{1,2,0:T(1,128)} %bitcast.16), calls=%async_computation.2 | async-start | bytes 4096 | tf_op jit(solution)/shard_map/all_to_all | solution.py:72
where the time goes:
time: 90.6 us; the launch traced here: 90.3 us
  blocking collectives  40 us (44%)
  waiting for transfers between devices  26.2 us (29%)
  starting transfers between devices  9.43 us (10%)
  other arithmetic  6 us (7%)
  local copies, waits for them, and re-layouts  4.95 us (5%)
  matrix products  3.59 us (4%)
    all_to_all x1, blocking collectives, per_device(): lax.all_to_all(send_rows, 'wide', split_axis=0, concat_axis=0, tiled=True)  31.9 us
    ppermute x6, waiting for transfers between devices, shifted(): lax.ppermute(shard, axis, [(i, (i + by) % count) for i in range(count)])  20.8 us
    all_to_all x1, blocking collectives, per_device(): lax.all_to_all(send_meta, 'wide', split_axis=0, concat_axis=0, tiled=True)  8.11 us
    ppermute x6, starting transfers between devices, shifted(): lax.ppermute(shard, axis, [(i, (i + by) % count) for i in range(count)])  6.05 us
    all_to_all x1, waiting for transfers between devices, per_device(): lax.all_to_all(best, 'wide', split_axis=0, concat_axis=0, tiled=True)  5.41 us
    dot_general x3, matrix products, pair_inner(): lax.dot_general(left, right, (((1,), (1,)), ((), ())), preferred_element_...  3.59 us
    all_to_all x1, starting transfers between devices, per_device(): lax.all_to_all(best, 'wide', split_axis=0, concat_axis=0, tiled=True)  3.38 us
    gather x1, local copies, waits for them, and re-layouts, per_device(): return answers[target]  2.5 us
  transfers between devices with their start and end apart: 7, of which 5 were waited for; matrix products, arithmetic and copies ran while one was open for 3% of the time, Pallas kernels for 0%

commit v1 on v0

--- a/solution.py
+++ b/solution.py
@@ -1,6 +1,8 @@
 import jax
 import jax.numpy as jnp
 from jax import lax
+from jax.experimental import pallas as pl
+from jax.experimental.pallas import tpu as pltpu
 from jax.sharding import PartitionSpec as P
 
 CPO = 16
@@ -73,9 +75,263 @@
     return answers[target]
 
 
+CHUNKS = 4
+MESH = pl.DeviceIdType.MESH
+
+
+def meet_kernel(emb, meta, out, qraw, uq, kbuf, ku, qmeta, kmeta, racc, rres, cacc, cres,
+                xs, xr, fs, fr, cs, cr, ms, mr, zs, zr, gs, zms, zmr, gms, rs, rr, ts, tr):
+    w = lax.axis_index("wide")
+    n = lax.axis_index("narrow")
+    core = lax.rem(n, 2)
+    near = n + 1 - 2 * core
+    cross = lax.rem(n + 2, 4)
+    far = lax.rem(near + 2, 4)
+    peers = (near, cross, far)
+    rows = emb.shape[0]
+    piece = rows // CHUNKS
+
+    def to_narrow(s, d, ss, rs_, who):
+        return pltpu.make_async_remote_copy(s, d, ss, rs_, device_id={"narrow": who}, device_id_type=MESH)
+
+    def to_wide(s, d, ss, rs_, who):
+        return pltpu.make_async_remote_copy(s, d, ss, rs_, device_id={"wide": who}, device_id_type=MESH)
+
+    barrier = pltpu.get_barrier_semaphore()
+    for who in peers:
+        pl.semaphore_signal(barrier, inc=1, device_id={"narrow": who}, device_id_type=MESH)
+    for hop in range(1, 4):
+        pl.semaphore_signal(barrier, inc=1, device_id={"wide": lax.rem(w + hop, 4)}, device_id_type=MESH)
+    pl.semaphore_wait(barrier, 6)
+
+    up = lax.rem(w + 1, 4)
+    down = lax.rem(w + 3, 4)
+    part = [pl.ds(c * piece, piece) for c in range(CHUNKS)]
+
+    own_z = [to_wide(emb.at[part[c]], kbuf.at[0, part[c]], zs.at[c], zr.at[0, c], up) for c in range(CHUNKS)]
+    own_zm = to_wide(meta, kmeta.at[0], zms, zmr.at[0], up)
+    last_z = [to_wide(emb.at[part[c]], kbuf.at[2, part[c]], zs.at[c], zr.at[2, c], down) for c in range(CHUNKS)]
+    last_zm = to_wide(meta, kmeta.at[2], zms, zmr.at[2], down)
+    one_z = [to_wide(kbuf.at[0, part[c]], kbuf.at[1, part[c]], gs.at[0, c], zr.at[1, c], up) for c in range(CHUNKS)]
+    one_zm = to_wide(kmeta.at[0], kmeta.at[1], gms.at[0], zmr.at[1], up)
+    two_z = [to_wide(kbuf.at[0, part[c]], kbuf.at[0, part[c]], gs.at[0, c], zr.at[0, c], up) for c in range(CHUNKS)]
+    two_zm = to_wide(kmeta.at[0], kmeta.at[0], gms.at[0], zmr.at[0], up)
+    sec_z = [to_wide(kbuf.at[1, part[c]], kbuf.at[1, part[c]], gs.at[1, c], zr.at[1, c], up) for c in range(CHUNKS)]
+    sec_zm = to_wide(kmeta.at[1], kmeta.at[1], gms.at[1], zmr.at[1], up)
+
+    @pl.when(w < 2)
+    def _():
+        own_zm.start()
+        for c in own_z:
+            c.start()
+
+    @pl.when(w == 3)
+    def _():
+        last_zm.start()
+        for c in last_z:
+            c.start()
+
+    met = [to_narrow(meta, qmeta.at[j], ms.at[j], mr.at[j], peers[j]) for j in range(3)]
+    xc = [to_narrow(emb.at[part[c]], qraw.at[1, part[c]], xs.at[c], xr.at[c], cross) for c in range(CHUNKS)]
+    cc = to_narrow(emb, qraw.at[0], cs, cr, near)
+    fc = [to_narrow(qraw.at[1, part[c]], qraw.at[2, part[c]], fs.at[c], fr.at[c], near) for c in range(CHUNKS)]
+    for c in met:
+        c.start()
+    for c in xc:
+        c.start()
+    cc.start()
+
+    def normed(ref):
+        values = ref[...].astype(jnp.float32)
+        return (values * lax.rsqrt(jnp.sum(values * values, axis=1, keepdims=True) + 1e-06)).astype(jnp.bfloat16)
+
+    def tall(row):
+        return jnp.broadcast_to(row, (rows, rows)).T
+
+    def own_part(j, code, base, q_meta):
+        inner = pair_inner(uq[0], uq[j])
+        ok = (base == q_meta[1:2]) & (code < q_meta[0:1])
+        racc[j] = jnp.max(jnp.where(ok, inner, -1.0), axis=0, keepdims=True)
+
+    def met_by(slot):
+        ku[...] = normed(kbuf.at[slot])
+        code = tall(kmeta[slot][0:1])
+        base = tall(kmeta[slot][1:2])
+        col = jnp.full((rows, rows), -1.0, jnp.float32)
+        for j in range(4):
+            q_meta = meta[...] if j == 0 else qmeta[j - 1]
+            inner = pair_inner(ku[...], uq[j])
+            same = jnp.where(base == q_meta[1:2], inner, -1.0)
+            before = code < q_meta[0:1]
+            racc[j] = jnp.maximum(racc[j], jnp.max(jnp.where(before, same, -1.0), axis=0, keepdims=True))
+            col = jnp.maximum(col, jnp.where(before, -1.0, same))
+        cacc[slot] = jnp.max(col.T, axis=0, keepdims=True)
+
+    uq[0] = normed(emb)
+    own_code = tall(meta[0:1])
+    own_base = tall(meta[1:2])
+    own_part(0, own_code, own_base, meta[...])
+    for c in met:
+        c.wait_recv()
+    cc.wait_recv()
+    uq[1] = normed(qraw.at[0])
+    own_part(1, own_code, own_base, qmeta[0])
+
+    @pl.when(w >= 1)
+    def _():
+        own_zm.wait_recv()
+
+    @pl.when(w == 1)
+    def _():
+        one_zm.start()
+
+    @pl.when(w == 2)
+    def _():
+        two_zm.start()
+
+    for c in range(CHUNKS):
+        @pl.when(w >= 1)
+        def _():
+            own_z[c].wait_recv()
+
+        @pl.when(w == 1)
+        def _():
+            one_z[c].start()
+
+        @pl.when(w == 2)
+        def _():
+            two_z[c].start()
+
+        xc[c].wait_recv()
+        fc[c].start()
+
+    uq[2] = normed(qraw.at[1])
+    own_part(2, own_code, own_base, qmeta[1])
+    for c in fc:
+        c.wait_recv()
+    uq[3] = normed(qraw.at[2])
+    own_part(3, own_code, own_base, qmeta[2])
+
+    back = [to_wide(cacc.at[s], cres.at[t], ts.at[s], tr.at[t], who)
+            for s, t, who in ((0, 0, 0), (0, 1, 1), (0, 2, 1), (1, 1, 0), (1, 2, 0), (2, 1, 3))]
+
+    @pl.when(w >= 1)
+    def _():
+        met_by(0)
+
+    @pl.when(w == 1)
+    def _():
+        back[0].start()
+
+    @pl.when(w == 2)
+    def _():
+        back[1].start()
+        last_zm.wait_recv()
+        for c in last_z:
+            c.wait_recv()
+        one_zm.wait_recv()
+        sec_zm.start()
+        for c in range(2):
+            one_z[c].wait_recv()
+            sec_z[c].start()
+        met_by(2)
+        back[5].start()
+        for c in range(2, CHUNKS):
+            one_z[c].wait_recv()
+            sec_z[c].start()
+        met_by(1)
+        back[3].start()
+
+    @pl.when(w == 3)
+    def _():
+        back[2].start()
+        sec_zm.wait_recv()
+        for c in sec_z:
+            c.wait_recv()
+        met_by(1)
+        back[4].start()
+
+    rowb = [to_narrow(racc.at[j + 1], rres.at[j], rs.at[j], rr.at[j], peers[j]) for j in range(3)]
+    for c in rowb:
+        c.start()
+    for c in rowb:
+        c.wait_recv()
+    out[...] = jnp.maximum(jnp.maximum(racc[0], rres[0]), jnp.maximum(rres[1], rres[2]))
+
+    @pl.when(w == 0)
+    def _():
+        for t in range(3):
+            back[(0, 3, 4)[t]].wait_recv()
+        out[...] = jnp.maximum(jnp.maximum(out[...], cres[0]), jnp.maximum(cres[1], cres[2]))
+        own_zm.wait_send()
+        for c in own_z:
+            c.wait_send()
+
+    @pl.when(w == 1)
+    def _():
+        back[1].wait_recv()
+        back[2].wait_recv()
+        out[...] = jnp.maximum(out[...], jnp.maximum(cres[1], cres[2]))
+        own_zm.wait_send()
+        one_zm.wait_send()
+        for c in own_z + one_z:
+            c.wait_send()
+        back[0].wait_send()
+
+    @pl.when(w == 2)
+    def _():
+        two_zm.wait_send()
+        sec_zm.wait_send()
+        for c in two_z + sec_z:
+            c.wait_send()
+        for i in (1, 5, 3):
+            back[i].wait_send()
+
+    @pl.when(w == 3)
+    def _():
+        back[5].wait_recv()
+        out[...] = jnp.maximum(out[...], cres[1])
+        last_zm.wait_send()
+        for c in last_z:
+            c.wait_send()
+        back[2].wait_send()
+        back[4].wait_send()
+
+    for c in met + xc + [cc] + fc + rowb:
+        c.wait_send()
+
+
+def per_device_meet(embeddings, cluster_id, order_index):
+    rows, width = embeddings.shape
+    total = rows * lax.axis_size("wide") * lax.axis_size("narrow")
+    base = cluster_id * total
+    meta = jnp.stack([base + order_index, base]).astype(jnp.float32)
+    dma = pltpu.SemaphoreType.DMA
+    vmem = pl.BlockSpec(memory_space=pltpu.VMEM)
+    wide_f = lambda k: pltpu.VMEM((k, 1, rows), jnp.float32)
+    block = lambda k: pltpu.VMEM((k, rows, width), jnp.bfloat16)
+    found = pl.pallas_call(
+        meet_kernel,
+        out_shape=jax.ShapeDtypeStruct((1, rows), jnp.float32),
+        in_specs=[vmem, vmem],
+        out_specs=vmem,
+        scratch_shapes=[
+            block(3), block(4), block(3), pltpu.VMEM((rows, width), jnp.bfloat16),
+            pltpu.VMEM((3, 2, rows), jnp.float32), pltpu.VMEM((3, 2, rows), jnp.float32),
+            wide_f(4), wide_f(3), wide_f(3), wide_f(3),
+            dma((CHUNKS,)), dma((CHUNKS,)), dma((CHUNKS,)), dma((CHUNKS,)), dma, dma, dma((3,)), dma((3,)),
+            dma((CHUNKS,)), dma((3, CHUNKS)), dma((2, CHUNKS)), dma, dma((3,)), dma((2,)),
+            dma((3,)), dma((3,)), dma((3,)), dma((3,)),
+        ],
+        compiler_params=pltpu.CompilerParams(collective_id=0, has_side_effects=True),
+    )(embeddings, meta)
+    return found.reshape(rows)
+
+
 def solution(mesh):
+    meet = mesh.shape["wide"] == 4 and mesh.shape["narrow"] == 4
     return jax.shard_map(
-        per_device,
+        per_device_meet if meet else per_device,
         mesh=mesh,
         in_specs=(
             P(("parts", "wide", "narrow"), None),

time: 90.6 us -> 44.1 us (0.49)
  Pallas kernels: 0 us -> 41.4 us
  blocking collectives: 40 us -> 0 us
  waiting for transfers between devices: 26.2 us -> 0 us
  starting transfers between devices: 9.43 us -> 0 us
  other arithmetic: 6 us -> 1.27 us
  local copies, waits for them, and re-layouts: 4.95 us -> 1.22 us
  matrix products: 3.59 us -> 0 us
    pallas_call x0 -> x1, Pallas kernels: none -> 41.4 us  [per_device_meet(): pl.pallas_call(meet_kernel, out_shape=jax.ShapeDtypeStruct((1, rows), jnp...]
    all_to_all x2 -> x0, blocking collectives: 40 us -> none  [the longest x1 31.9 us: per_device(): lax.all_to_all(send_rows, 'wide', split_axis=0, concat_axis=0, tiled=True)]
    ppermute x6 -> x0, waiting for transfers between devices: 20.8 us -> none  [shifted(): lax.ppermute(shard, axis, [(i, (i + by) % count) for i in range(count)])]
    ppermute x6 -> x0, starting transfers between devices: 6.05 us -> none  [shifted(): lax.ppermute(shard, axis, [(i, (i + by) % count) for i in range(count)])]
    all_to_all x1 -> x0, waiting for transfers between devices: 5.41 us -> none  [per_device(): lax.all_to_all(best, 'wide', split_axis=0, concat_axis=0, tiled=True)]
    dot_general x3 -> x0, matrix products: 3.59 us -> none  [pair_inner(): lax.dot_general(left, right, (((1,), (1,)), ((), ())), preferred_element_...]
    all_to_all x1 -> x0, starting transfers between devices: 3.38 us -> none  [per_device(): lax.all_to_all(best, 'wide', split_axis=0, concat_axis=0, tiled=True)]
    gather x1 -> x0, local copies, waits for them, and re-layouts: 2.5 us -> none  [per_device(): return answers[target]]
  transfers between devices with their start and end apart: 7 -> 0, of which waited for: 5 -> 0; matrix products, arithmetic and copies ran while one was open for 3% -> 0% of each run, Pallas kernels for 0% -> 0%
where the time goes in v1:
time: 44.1 us; the launch traced here: 43.9 us
  Pallas kernels  41.4 us (94%)
  other arithmetic  1.27 us (3%)
  local copies, waits for them, and re-layouts  1.22 us (3%)
    pallas_call x1, Pallas kernels, per_device_meet(): pl.pallas_call(meet_kernel, out_shape=jax.ShapeDtypeStruct((1, rows), jnp...  41.4 us
    unnamed x3, local copies, waits for them, and re-layouts  1.22 us

profile of v1, /device:TPU:0, one launch (start us, length us, event | category | flops | bytes accessed | tf_op | source)
XLA Modules:
  0.0 43.9 jit_solution(10603884494366634454)
XLA Ops:
  0.0 0.7 %fusion = (s32[256]{0:T(256)S(1)}, s32[256]{0:T(256)S(1)}) fusion(s32[256]{0:T(256)} %param.5, s32[256]{0:T(256)} %param.4), kind=kLoop, calls=%fused_computation.2 | loop fusion | flops 512 | bytes 4096 | tf_op jit(solution)/shard_map/add | solution.py:308
  0.7 0.6 %add_convert_fusion.meta = f32[2,256]{1,0:T(2,128)} fusion(s32[1,256]{1,0:T(1,128)S(1)} %bitcast.5, s32[1,256]{1,0:T(1,128)S(1)} %bitcast.4), kind=kLoop, calls=%fused_computation | loop fusion | flops 1024 | bytes 4096 | tf_op jit(solution)/shard_map/convert_element_type | solution.py:308
  1.3 41.4 %shard_map.37 = f32[1,256]{1,0:T(1,128)} custom-call(bf16[256,1024]{1,0:T(8,128)(2,1)} %emb.1, f32[2,256]{1,0:T(2,128)} %add_convert_fusion.meta), custom_call_target="tpu_custom_call" | custom-call | tf_op jit(solution)/shard_map/pallas_call | solution.py:313
  42.7 0.0 copy-start
  42.7 0.7 %copy-done = f32[1,256]{1,0:T(1,128)S(1)} copy-done((f32[1,256]{1,0:T(1,128)S(1)}, f32[1,256]{1,0:T(1,128)}, u32[]{:S(2)}) %copy-start) | copy-done | bytes 1048
  43.4 0.6 %copy.5 = f32[256]{0:T(256)} copy(f32[256]{0:T(256)S(1)} %bitcast.3) | data formatting | bytes 2048
Async XLA Ops:
  42.7 0.7 %copy-start = (f32[1,256]{1,0:T(1,128)S(1)}, f32[1,256]{1,0:T(1,128)}, u32[]{:S(2)}) copy-start(f32[1,256]{1,0:T(1,128)} %shard_map.37) | copy-start | bytes 3076

commit v2 on v0

--- a/solution.py
+++ b/solution.py
@@ -1,6 +1,8 @@
 import jax
 import jax.numpy as jnp
 from jax import lax
+from jax.experimental import pallas as pl
+from jax.experimental.pallas import tpu as pltpu
 from jax.sharding import PartitionSpec as P
 
 CPO = 16
@@ -73,9 +75,302 @@
     return answers[target]
 
 
+CHUNKS = 4
+SIDE = 4
+MESH = pl.DeviceIdType.MESH
+
+
+def meet_kernel(emb, cl, od, out, qraw, uq, acl, qod, pk, pm, kbuf, kmeta, target, racc, rres, cacc, cres, cfull,
+                xs, xr, fs, fr, cs, cr, als, alr, ods, odr, zs, zr, zms, zmr, rs, rr, ts, tr):
+    w = lax.axis_index("wide")
+    n = lax.axis_index("narrow")
+    near = n + 1 - 2 * lax.rem(n, 2)
+    cross = lax.rem(n + 2, SIDE)
+    far = lax.rem(near + 2, SIDE)
+    peers = (near, cross, far)
+    mate = w + 1 - 2 * lax.rem(w, 2)
+    over = SIDE - 1 - w
+    over_mate = over + 1 - 2 * lax.rem(over, 2)
+    outer = (w == 0) | (w == SIDE - 1)
+    inner = (w > 0) & (w < SIDE - 1)
+    rows = emb.shape[0]
+    half = rows // 2
+    f32 = jnp.float32
+
+    def send(s, d, ss, rs_, **who):
+        return pltpu.make_async_remote_copy(s, d, ss, rs_, device_id=who, device_id_type=MESH)
+
+    others = [(a, b) for a in range(SIDE) for b in range(SIDE) if a or b]
+    barrier = pltpu.get_barrier_semaphore()
+    for a, b in others:
+        pl.semaphore_signal(
+            barrier, inc=1, device_id={"wide": lax.rem(w + a, SIDE), "narrow": lax.rem(n + b, SIDE)}, device_id_type=MESH
+        )
+    pl.semaphore_wait(barrier, len(others))
+
+    x_part = [pl.ds(c * (rows // CHUNKS), rows // CHUNKS) for c in range(CHUNKS)]
+    z_part = [pl.ds(c * (half // CHUNKS), half // CHUNKS) for c in range(CHUNKS)]
+
+    ids = [
+        send(cl, acl.at[a * SIDE + b], als.at[a * SIDE + b], alr.at[a * SIDE + b],
+             wide=lax.rem(w + a, SIDE), narrow=lax.rem(n + b, SIDE))
+        for a, b in others
+    ]
+    orders = [send(od, qod.at[b - 1], ods.at[b - 1], odr.at[b - 1], narrow=lax.rem(n + b, SIDE)) for b in range(1, SIDE)]
+    xc = [send(emb.at[p], qraw.at[1, p], xs.at[c], xr.at[c], narrow=cross) for c, p in enumerate(x_part)]
+    cc = send(emb, qraw.at[0], cs, cr, narrow=near)
+    fc = [send(qraw.at[1, p], qraw.at[2, p], fs.at[c], fr.at[c], narrow=near) for c, p in enumerate(x_part)]
+    for c in ids[::-1] + orders + [cc] + xc:
+        c.start()
+
+    def normed(ref):
+        values = ref[...].astype(f32)
+        return (values * lax.rsqrt(jnp.sum(values * values, axis=1, keepdims=True) + 1e-06)).astype(jnp.bfloat16)
+
+    def tall(row, across):
+        return jnp.broadcast_to(row, (across, row.shape[1])).T
+
+    def asked(j):
+        if j == 0:
+            return cl[...].astype(f32), od[...].astype(f32)
+        if j == 2:
+            return acl[2].astype(f32), qod[1].astype(f32)
+        even = lax.rem(n, 2) == 0
+        low, high = (3, 1) if j == 1 else (1, 3)
+        slot = jnp.where(even, low, high)
+        return acl[slot].astype(f32), qod[slot - 1].astype(f32)
+
+    uq[0] = normed(emb)
+    own_cl = tall(cl[...].astype(f32), rows)
+    own_od = tall(od[...].astype(f32), rows)
+
+    def own_part(j):
+        q_cl, q_od = asked(j)
+        ok = (own_cl == q_cl) & (own_od < q_od)
+        racc[j] = jnp.max(jnp.where(ok, pair_inner(uq[0], uq[j]), -1.0), axis=0, keepdims=True)
+
+    own_part(0)
+    acl[0] = cl[...]
+    for c in ids + orders:
+        c.wait_recv()
+
+    all_cl = acl[...].astype(f32)
+    full = jnp.zeros((1, 1), f32)
+    for o in range(SIDE)[::-1]:
+        mine = (all_cl >= o * CPO) & (all_cl < (o + 1) * CPO)
+        count = jnp.sum(jnp.where(mine, 1.0, 0.0), axis=2, keepdims=True)
+        good = jnp.min(jnp.where(count == half, 1.0, 0.0), axis=0)
+        full = jnp.where(good > 0.5, jnp.float32(o), full)
+    id_row = cl[...].astype(f32)
+    od_row = od[...].astype(f32)
+    heavy = jnp.where((id_row >= full * CPO) & (id_row < (full + 1.0) * CPO), 1.0, 0.0)
+    away = jnp.where(w < SIDE // 2, heavy, 1.0 - heavy)
+    deep = lax.broadcasted_iota(jnp.int32, (rows, rows), 0)
+    long = lax.broadcasted_iota(jnp.int32, (rows, rows), 1)
+    tri = jnp.where(deep < long, 1.0, 0.0).astype(jnp.bfloat16)
+    rank = jnp.dot(jnp.broadcast_to(away, (16, rows)).astype(jnp.bfloat16), tri, preferred_element_type=f32)[0:1]
+    lane = lax.broadcasted_iota(jnp.int32, (1, rows), 1).astype(f32)
+    place = jnp.where(away > 0.5, rank, half + lane - rank)
+    target[...] = place
+    pick = jnp.where(deep.astype(f32) == place, 1.0, 0.0).astype(jnp.bfloat16)
+    od_high = jnp.floor(od_row * (1.0 / 128))
+    od_low = od_row - od_high * 128
+    tags = [jnp.broadcast_to(r, (16, rows)).astype(jnp.bfloat16) for r in (id_row, od_high, od_low)]
+    tagged = [pair_inner(t, pick)[0:1] for t in tags]
+    moved = jnp.concatenate([tagged[0], tagged[1] * 128 + tagged[2]], axis=0)
+    pm[0] = moved[:, :half]
+    pm[1] = moved[:, half:]
+    for s in range(2):
+        pk[s] = jnp.dot(pick[s * half:(s + 1) * half], uq[0], preferred_element_type=f32).astype(jnp.bfloat16)
+
+    def row_of(src, dst, ss, slot, who):
+        return [send(src.at[p], kbuf.at[dst, p], zs.at[ss, c], zr.at[slot, c], wide=who) for c, p in enumerate(z_part)]
+
+    out_away = row_of(pk.at[0], 2, 0, 2, mate)
+    out_home = row_of(pk.at[1], 3, 1, 3, mate)
+    in_away = row_of(pk.at[0], 0, 0, 0, over)
+    in_next = row_of(kbuf.at[2], 1, 1, 1, over)
+    on_near = row_of(kbuf.at[0], 0, 2, 0, mate)
+    on_far = row_of(kbuf.at[1], 1, 3, 1, mate)
+
+    def tag_of(src, dst, ss, who):
+        return send(src, kmeta.at[dst], zms.at[ss], zmr.at[dst], wide=who)
+
+    t_out_away = tag_of(pm.at[0], 2, 0, mate)
+    t_out_home = tag_of(pm.at[1], 3, 1, mate)
+    t_in_away = tag_of(pm.at[0], 0, 0, over)
+    t_in_next = tag_of(kmeta.at[2], 1, 1, over)
+    t_on_near = tag_of(kmeta.at[0], 0, 2, mate)
+    t_on_far = tag_of(kmeta.at[1], 1, 3, mate)
+
+    @pl.when(outer)
+    def _():
+        t_out_away.start()
+        t_out_home.start()
+        for c in out_away + out_home:
+            c.start()
+
+    @pl.when(inner)
+    def _():
+        t_in_away.start()
+        for c in in_away:
+            c.start()
+
+    cc.wait_recv()
+    uq[1] = normed(qraw.at[0])
+    own_part(1)
+
+    @pl.when(inner)
+    def _():
+        t_out_away.wait_recv()
+        t_in_next.start()
+        t_in_away.wait_recv()
+        t_on_near.start()
+
+    for c in range(CHUNKS):
+        xc[c].wait_recv()
+        fc[c].start()
+
+        @pl.when(inner)
+        def _():
+            out_away[c].wait_recv()
+            in_next[c].start()
+            in_away[c].wait_recv()
+            on_near[c].start()
+
+    uq[2] = normed(qraw.at[1])
+    own_part(2)
+
+    @pl.when(inner)
+    def _():
+        t_in_next.wait_recv()
+        t_on_far.start()
+        in_next[0].wait_recv()
+        on_far[0].start()
+
+    for c in fc:
+        c.wait_recv()
+    uq[3] = normed(qraw.at[2])
+    own_part(3)
+
+    def met_by(slot):
+        k_cl = tall(kmeta[slot][0:1], rows)
+        k_od = tall(kmeta[slot][1:2], rows)
+        col = jnp.full((half, rows), -1.0, f32)
+        for j in range(4):
+            q_cl, q_od = asked(j)
+            same = jnp.where(k_cl == q_cl, pair_inner(kbuf[slot], uq[j]), -1.0)
+            before = k_od < q_od
+            racc[j] = jnp.maximum(racc[j], jnp.max(jnp.where(before, same, -1.0), axis=0, keepdims=True))
+            col = jnp.maximum(col, jnp.where(before, -1.0, same))
+        cacc[slot] = jnp.max(col.T, axis=0, keepdims=True)
+
+    def back(slot, dst, who):
+        return send(cacc.at[slot], cres.at[dst], ts.at[slot], tr.at[dst], wide=who)
+
+    b_in = [back(0, 0, over), back(1, 0, over_mate), back(2, 2, mate), back(3, 3, mate)]
+    b_out = [back(0, 1, over_mate), back(1, 1, over)]
+
+    @pl.when(inner)
+    def _():
+        in_next[1].wait_recv()
+        on_far[1].start()
+        met_by(0)
+        b_in[0].start()
+        for c in range(2, CHUNKS):
+            in_next[c].wait_recv()
+            on_far[c].start()
+        met_by(1)
+        b_in[1].start()
+        t_out_home.wait_recv()
+        for c in out_home:
+            c.wait_recv()
+        met_by(2)
+        b_in[2].start()
+        met_by(3)
+        b_in[3].start()
+
+    @pl.when(outer)
+    def _():
+        t_on_near.wait_recv()
+        for c in on_near:
+            c.wait_recv()
+        met_by(0)
+        b_out[0].start()
+        t_on_far.wait_recv()
+        for c in on_far:
+            c.wait_recv()
+        met_by(1)
+        b_out[1].start()
+
+    rowb = [send(racc.at[j + 1], rres.at[j], rs.at[j], rr.at[j], narrow=peers[j]) for j in range(3)]
+    for c in rowb:
+        c.start()
+    for c in rowb:
+        c.wait_recv()
+    b_in[0].wait_recv()
+    b_out[0].wait_recv()
+    cfull[:, :half] = jnp.maximum(cres[0], cres[1])
+    cfull[:, half:] = jnp.full((1, half), -1.0, f32)
+
+    @pl.when(outer)
+    def _():
+        b_in[2].wait_recv()
+        b_in[3].wait_recv()
+        cfull[:, :half] = jnp.maximum(cfull[:, :half], cres[2])
+        cfull[:, half:] = cres[3]
+
+    mine = jnp.where(deep.astype(f32) == target[...], tall(cfull[...], rows), -1.0)
+    best = jnp.maximum(jnp.maximum(racc[0], rres[0]), jnp.maximum(rres[1], rres[2]))
+    out[...] = jnp.maximum(best, jnp.max(mine, axis=0, keepdims=True))
+
+    @pl.when(outer)
+    def _():
+        for c in [t_out_away, t_out_home] + out_away + out_home + b_out:
+            c.wait_send()
+
+    @pl.when(inner)
+    def _():
+        for c in [t_in_away, t_in_next, t_on_near, t_on_far] + in_away + in_next + on_near + on_far + b_in:
+            c.wait_send()
+
+    for c in ids + orders + xc + [cc] + fc + rowb:
+        c.wait_send()
+
+
+def per_device_meet(embeddings, cluster_id, order_index):
+    rows, width = embeddings.shape
+    half = rows // 2
+    dma = pltpu.SemaphoreType.DMA
+    vmem = pl.BlockSpec(memory_space=pltpu.VMEM)
+    line = lambda k, m: pltpu.VMEM((k, 1, m), jnp.float32)
+    block = lambda k, m: pltpu.VMEM((k, m, width), jnp.bfloat16)
+    found = pl.pallas_call(
+        meet_kernel,
+        out_shape=jax.ShapeDtypeStruct((1, rows), jnp.float32),
+        in_specs=[vmem, vmem, vmem],
+        out_specs=vmem,
+        scratch_shapes=[
+            block(3, rows), block(4, rows),
+            pltpu.VMEM((SIDE * SIDE, 1, rows), jnp.int32), pltpu.VMEM((3, 1, rows), jnp.int32),
+            block(2, half), pltpu.VMEM((2, 2, half), jnp.float32),
+            block(4, half), pltpu.VMEM((4, 2, half), jnp.float32),
+            pltpu.VMEM((1, rows), jnp.float32),
+            line(4, rows), line(3, rows), line(4, half), line(4, half), pltpu.VMEM((1, rows), jnp.float32),
+            dma((CHUNKS,)), dma((CHUNKS,)), dma((CHUNKS,)), dma((CHUNKS,)), dma, dma,
+            dma((SIDE * SIDE,)), dma((SIDE * SIDE,)), dma((3,)), dma((3,)),
+            dma((4, CHUNKS)), dma((4, CHUNKS)), dma((4,)), dma((4,)),
+            dma((3,)), dma((3,)), dma((4,)), dma((4,)),
+        ],
+        compiler_params=pltpu.CompilerParams(collective_id=0, has_side_effects=True),
+    )(embeddings, cluster_id.reshape(1, rows), order_index.reshape(1, rows))
+    return jnp.maximum(found.reshape(rows), -1.0)
+
+
 def solution(mesh):
+    meet = mesh.shape["wide"] == SIDE and mesh.shape["narrow"] == SIDE
     return jax.shard_map(
-        per_device,
+        per_device_meet if meet else per_device,
         mesh=mesh,
         in_specs=(
             P(("parts", "wide", "narrow"), None),

time: 90.6 us -> 35.9 us (0.40)
  blocking collectives: 40 us -> 0 us
  Pallas kernels: 0 us -> 34.5 us
  waiting for transfers between devices: 26.2 us -> 0 us
  starting transfers between devices: 9.43 us -> 0 us
  local copies, waits for them, and re-layouts: 4.95 us -> 0 us
  other arithmetic: 6 us -> 1.24 us
  matrix products: 3.59 us -> 0 us
    all_to_all x2 -> x0, blocking collectives: 40 us -> none  [the longest x1 31.9 us: per_device(): lax.all_to_all(send_rows, 'wide', split_axis=0, concat_axis=0, tiled=True)]
    pallas_call x0 -> x1, Pallas kernels: none -> 34.5 us  [per_device_meet(): pl.pallas_call(meet_kernel, out_shape=jax.ShapeDtypeStruct((1, rows), jnp...]
    ppermute x6 -> x0, waiting for transfers between devices: 20.8 us -> none  [shifted(): lax.ppermute(shard, axis, [(i, (i + by) % count) for i in range(count)])]
    ppermute x6 -> x0, starting transfers between devices: 6.05 us -> none  [shifted(): lax.ppermute(shard, axis, [(i, (i + by) % count) for i in range(count)])]
    all_to_all x1 -> x0, waiting for transfers between devices: 5.41 us -> none  [per_device(): lax.all_to_all(best, 'wide', split_axis=0, concat_axis=0, tiled=True)]
    dot_general x3 -> x0, matrix products: 3.59 us -> none  [pair_inner(): lax.dot_general(left, right, (((1,), (1,)), ((), ())), preferred_element_...]
    all_to_all x1 -> x0, starting transfers between devices: 3.38 us -> none  [per_device(): lax.all_to_all(best, 'wide', split_axis=0, concat_axis=0, tiled=True)]
    gather x1 -> x0, local copies, waits for them, and re-layouts: 2.5 us -> none  [per_device(): return answers[target]]
  transfers between devices with their start and end apart: 7 -> 0, of which waited for: 5 -> 0; matrix products, arithmetic and copies ran while one was open for 3% -> 0% of each run, Pallas kernels for 0% -> 0%
where the time goes in v2:
time: 35.9 us; the launch traced here: 35.7 us
  Pallas kernels  34.5 us (96%)
  other arithmetic  1.24 us (3%)
    pallas_call x1, Pallas kernels, per_device_meet(): pl.pallas_call(meet_kernel, out_shape=jax.ShapeDtypeStruct((1, rows), jnp...  34.5 us
    max x1, other arithmetic, per_device_meet(): return jnp.maximum(found.reshape(rows), -1.0)  1.24 us

profile of v2, /device:TPU:0, one launch (start us, length us, event | category | flops | bytes accessed | tf_op | source)
XLA Modules:
  0.0 35.7 jit_solution(14198469950647183110)
XLA Ops:
  0.0 34.5 %shard_map.37 = f32[1,256]{1,0:T(1,128)} custom-call(bf16[256,1024]{1,0:T(8,128)(2,1)} %emb.1, s32[1,256]{1,0:T(1,128)} %bitcast.3, s32[1,256]{1,0:T(1,128)} %bitcast.4), custom_call_target="tpu_custom_call" | custom-call | tf_op jit(solution)/shard_map/pallas_call | solution.py:348
  34.5 1.2 %broadcast_maximum_fusion = f32[1,256]{1,0:T(1,128)} fusion(f32[1,256]{1,0:T(1,128)} %shard_map.37), kind=kLoop, calls=%fused_computation | loop fusion | flops 256 | bytes 2048 | tf_op jit(solution)/shard_map/max | solution.py:367

commit v3 on v2

--- a/solution.py
+++ b/solution.py
@@ -80,7 +80,7 @@
 MESH = pl.DeviceIdType.MESH
 
 
-def meet_kernel(emb, cl, od, out, qraw, uq, acl, qod, pk, pm, kbuf, kmeta, target, racc, rres, cacc, cres, cfull,
+def meet_kernel(emb_far, cl, od, out, emb, got, qraw, uq, acl, qod, pk, pm, kbuf, kmeta, target, racc, rres, cacc, cres, cfull,
                 xs, xr, fs, fr, cs, cr, als, alr, ods, odr, zs, zr, zms, zmr, rs, rr, ts, tr):
     w = lax.axis_index("wide")
     n = lax.axis_index("narrow")
@@ -106,6 +106,8 @@
         pl.semaphore_signal(
             barrier, inc=1, device_id={"wide": lax.rem(w + a, SIDE), "narrow": lax.rem(n + b, SIDE)}, device_id_type=MESH
         )
+    take = pltpu.make_async_copy(emb_far, emb, got)
+    take.start()
     pl.semaphore_wait(barrier, len(others))
 
     x_part = [pl.ds(c * (rows // CHUNKS), rows // CHUNKS) for c in range(CHUNKS)]
@@ -120,7 +122,10 @@
     xc = [send(emb.at[p], qraw.at[1, p], xs.at[c], xr.at[c], narrow=cross) for c, p in enumerate(x_part)]
     cc = send(emb, qraw.at[0], cs, cr, narrow=near)
     fc = [send(qraw.at[1, p], qraw.at[2, p], fs.at[c], fr.at[c], narrow=near) for c, p in enumerate(x_part)]
-    for c in ids[::-1] + orders + [cc] + xc:
+    for c in ids[::-1] + orders:
+        c.start()
+    take.wait()
+    for c in xc + [cc]:
         c.start()
 
     def normed(ref):
@@ -348,10 +353,10 @@
     found = pl.pallas_call(
         meet_kernel,
         out_shape=jax.ShapeDtypeStruct((1, rows), jnp.float32),
-        in_specs=[vmem, vmem, vmem],
+        in_specs=[pl.BlockSpec(memory_space=pl.ANY), vmem, vmem],
         out_specs=vmem,
         scratch_shapes=[
-            block(3, rows), block(4, rows),
+            pltpu.VMEM((rows, width), jnp.bfloat16), dma, block(3, rows), block(4, rows),
             pltpu.VMEM((SIDE * SIDE, 1, rows), jnp.int32), pltpu.VMEM((3, 1, rows), jnp.int32),
             block(2, half), pltpu.VMEM((2, 2, half), jnp.float32),
             block(4, half), pltpu.VMEM((4, 2, half), jnp.float32),

time: 35.9 us -> 35.6 us (level)
  Pallas kernels: 34.5 us -> 34.1 us
where the time goes in v3:
time: 35.6 us; the launch traced here: 35.4 us
  Pallas kernels  34.1 us (96%)
  other arithmetic  1.24 us (3%)
    pallas_call x1, Pallas kernels, per_device_meet(): pl.pallas_call(meet_kernel, out_shape=jax.ShapeDtypeStruct((1, rows), jnp...  34.1 us
    max x1, other arithmetic, per_device_meet(): return jnp.maximum(found.reshape(rows), -1.0)  1.24 us

profile of v3, /device:TPU:0, one launch (start us, length us, event | category | flops | bytes accessed | tf_op | source)
XLA Modules:
  0.0 35.4 jit_solution(9779058940642202072)
XLA Ops:
  0.0 34.1 %shard_map.37 = f32[1,256]{1,0:T(1,128)} custom-call(bf16[256,1024]{1,0:T(8,128)(2,1)} %emb_far.1, s32[1,256]{1,0:T(1,128)} %bitcast.3, s32[1,256]{1,0:T(1,128)} %bitcast.4), custom_call_target="tpu_custom_call" | custom-call | tf_op jit(solution)/shard_map/pallas_call | solution.py:353
  34.1 1.2 %broadcast_maximum_fusion = f32[1,256]{1,0:T(1,128)} fusion(f32[1,256]{1,0:T(1,128)} %shard_map.37), kind=kLoop, calls=%fused_computation | loop fusion | flops 256 | bytes 2048 | tf_op jit(solution)/shard_map/max | solution.py:372

commit v4 on v3

--- a/solution.py
+++ b/solution.py
@@ -258,17 +258,26 @@
     uq[3] = normed(qraw.at[2])
     own_part(3)
 
-    def met_by(slot):
+    def met_by(slot, ready=None):
         k_cl = tall(kmeta[slot][0:1], rows)
         k_od = tall(kmeta[slot][1:2], rows)
-        col = jnp.full((half, rows), -1.0, f32)
-        for j in range(4):
-            q_cl, q_od = asked(j)
-            same = jnp.where(k_cl == q_cl, pair_inner(kbuf[slot], uq[j]), -1.0)
-            before = k_od < q_od
-            racc[j] = jnp.maximum(racc[j], jnp.max(jnp.where(before, same, -1.0), axis=0, keepdims=True))
-            col = jnp.maximum(col, jnp.where(before, -1.0, same))
-        cacc[slot] = jnp.max(col.T, axis=0, keepdims=True)
+        quarter = half // 2
+        cols = []
+        for b in range(2):
+            if ready is not None:
+                for c in ready[b * CHUNKS // 2:(b + 1) * CHUNKS // 2]:
+                    c.wait_recv()
+            span = slice(b * quarter, (b + 1) * quarter)
+            keys = kbuf[slot, span]
+            col = jnp.full((quarter, rows), -1.0, f32)
+            for j in range(4):
+                q_cl, q_od = asked(j)
+                same = jnp.where(k_cl[span] == q_cl, pair_inner(keys, uq[j]), -1.0)
+                before = k_od[span] < q_od
+                racc[j] = jnp.maximum(racc[j], jnp.max(jnp.where(before, same, -1.0), axis=0, keepdims=True))
+                col = jnp.maximum(col, jnp.where(before, -1.0, same))
+            cols.append(col)
+        cacc[slot] = jnp.max(jnp.concatenate(cols, axis=0).T, axis=0, keepdims=True)
 
     def back(slot, dst, who):
         return send(cacc.at[slot], cres.at[dst], ts.at[slot], tr.at[dst], wide=who)
@@ -303,9 +312,7 @@
         met_by(0)
         b_out[0].start()
         t_on_far.wait_recv()
-        for c in on_far:
-            c.wait_recv()
-        met_by(1)
+        met_by(1, on_far)
         b_out[1].start()
 
     rowb = [send(racc.at[j + 1], rres.at[j], rs.at[j], rr.at[j], narrow=peers[j]) for j in range(3)]

time: 35.6 us -> 35.5 us (level)
  no operation moved by 1% of the time
where the time goes in v4:
time: 35.5 us; the launch traced here: 35.3 us
  Pallas kernels  34 us (96%)
  other arithmetic  1.24 us (3%)
    pallas_call x1, Pallas kernels, per_device_meet(): pl.pallas_call(meet_kernel, out_shape=jax.ShapeDtypeStruct((1, rows), jnp...  34 us
    max x1, other arithmetic, per_device_meet(): return jnp.maximum(found.reshape(rows), -1.0)  1.24 us

profile of v4, /device:TPU:0, one launch (start us, length us, event | category | flops | bytes accessed | tf_op | source)
XLA Modules:
  0.0 35.3 jit_solution(6305211902439716467)
XLA Ops:
  0.0 34.0 %shard_map.37 = f32[1,256]{1,0:T(1,128)} custom-call(bf16[256,1024]{1,0:T(8,128)(2,1)} %emb_far.1, s32[1,256]{1,0:T(1,128)} %bitcast.3, s32[1,256]{1,0:T(1,128)} %bitcast.4), custom_call_target="tpu_custom_call" | custom-call | tf_op jit(solution)/shard_map/pallas_call | solution.py:360
  34.1 1.2 %broadcast_maximum_fusion = f32[1,256]{1,0:T(1,128)} fusion(f32[1,256]{1,0:T(1,128)} %shard_map.37), kind=kLoop, calls=%fused_computation | loop fusion | flops 256 | bytes 2048 | tf_op jit(solution)/shard_map/max | solution.py:379
